TPU v7x, 32 devices: a whole 2x2x4 slice. The times are simulated.
32 devices in a mesh: groups: 1, kcol: 16 (over z, y, x), qrow: 2 (over core).
Axes of the slice: x: 2, y: 2, z: 4, core: 2. Of those that a mesh axis runs over, the one named last changes fastest.
Arguments:
- queries: bfloat16 [128, 1024], P(('groups', 'kcol', 'qrow')), may hold values from -120 to 120
- key_value: bfloat16 [24576, 256], P(('groups', 'kcol')), may hold values from -6 to 6
- block_lists: int32 [1, 64], P('groups'), may hold values from 0 to 191, as said below
Outputs:
- attended: bfloat16 [128, 1024], P(('groups', 'kcol', 'qrow'))
Inputs may be any that keep to these rules, and one draw needn't show every extreme that they name: `block_lists`: row i names 64 distinct key blocks, none after block 191 + i (the block that holds query block i); it always names that block, the 11 blocks just before it, and block 0.
All inputs are finite; a program needn't handle non-finite values.
Results may differ from a plain program's by a relative error of at most 0.0065.
Values may be sent and summed in bfloat16 or wider, within the bound.
No kernel may reach another device: no remote copies, remote signals or barrier semaphores. Data moves between devices by JAX's collectives and lax.ppermute only.
A program may use at most 128 MiB of HBM per device.

v0:
```python
import math
import jax
import jax.numpy as jnp
from jax import lax
from jax.sharding import PartitionSpec as P

BLK = 128
masked_score = -1e30


def combined_all(part, axis, combine):
    gathered = jax.tree.map(lambda a: lax.all_gather(a, axis), part)

    def take(source):
        return jax.tree.map(lambda a: lax.dynamic_index_in_dim(a, source, 0, False), gathered)

    return lax.fori_loop(
        1, lax.axis_size(axis), lambda source, state: combine(state, take(source)), take(0)
    )


def partial_softmax(query_tile, key_rows, value_rows, visible):
    score_scale = 1.0 / math.sqrt(key_rows.shape[1])
    scores = (
        jnp.einsum("thd,kd->htk", query_tile, key_rows, preferred_element_type=jnp.float32)
        * score_scale
    )
    scores = jnp.where(visible[None], scores, masked_score)
    row_max = jnp.max(scores, axis=-1)
    weights = jnp.where(visible[None], jnp.exp(scores - row_max[..., None]), 0.0)
    row_total = jnp.sum(weights, axis=-1)
    numerator = jnp.einsum(
        "htk,kd->thd", weights.astype(jnp.bfloat16), value_rows, preferred_element_type=jnp.float32
    )
    return (jnp.transpose(row_max), jnp.transpose(row_total), numerator)


def combine_partials(left_part, right_part):
    max_left, total_left, numer_left = left_part
    max_right, total_right, numer_right = right_part
    row_max = jnp.maximum(max_left, max_right)
    scale_left = jnp.exp(max_left - row_max)
    scale_right = jnp.exp(max_right - row_max)
    return (
        row_max,
        total_left * scale_left + total_right * scale_right,
        numer_left * scale_left[..., None] + numer_right * scale_right[..., None],
    )


def per_device(queries, key_value, block_lists):
    column_count = lax.axis_size("kcol")
    column = lax.axis_index("kcol")
    row_count = lax.axis_size("qrow")
    row_index = lax.axis_index("qrow")
    tok_dev = queries.shape[0]
    feature_count = queries.shape[1]
    head_dim = key_value.shape[1] // 2
    head_count = feature_count // head_dim
    stored = key_value.shape[0] // BLK
    all_blocks = stored * column_count
    gathered = lax.all_gather(queries, "kcol", axis=0, tiled=True)
    gathered_rows = gathered.shape[0]
    tile_rows = BLK // row_count
    query_blocks = gathered_rows // tile_rows
    offset = (all_blocks - query_blocks) * BLK
    gather_pos = jnp.arange(gathered_rows, dtype=jnp.int32)
    token_index = (gather_pos // tok_dev * row_count + row_index) * tok_dev + gather_pos % tok_dev
    query_pos = (offset + token_index).reshape(query_blocks, tile_rows)
    query_tiles = gathered.reshape(query_blocks, tile_rows, head_count, head_dim)
    block_ids = column * stored + jnp.arange(stored, dtype=jnp.int32)
    key_pos = column * stored * BLK + jnp.arange(stored * BLK, dtype=jnp.int32)
    key_rows = key_value[:, :head_dim]
    value_rows = key_value[:, head_dim:]

    def one_block(inputs):
        query_tile, positions, listed = inputs
        listed_here = jnp.any(listed[:, None] == block_ids[None, :], axis=0)
        usable = jnp.repeat(listed_here, BLK, total_repeat_length=stored * BLK)
        visible = usable[None, :] & (key_pos[None, :] <= positions[:, None])
        return partial_softmax(query_tile, key_rows, value_rows, visible)

    row_max, row_total, numerator = lax.map(one_block, (query_tiles, query_pos, block_lists))
    row_max = row_max.reshape(gathered_rows, head_count)
    row_total = row_total.reshape(gathered_rows, head_count)
    numerator = numerator.reshape(gathered_rows, head_count, head_dim)
    merged = combined_all((row_max, row_total, numerator), "kcol", combine_partials)
    first_row = column * tok_dev
    summed_total = lax.dynamic_slice_in_dim(merged[1], first_row, tok_dev, 0)
    summed_numer = lax.dynamic_slice_in_dim(merged[2], first_row, tok_dev, 0)
    attended = summed_numer / summed_total[..., None]
    return attended.reshape(tok_dev, feature_count).astype(jnp.bfloat16)


def solution(mesh):
    placed = (P(("groups", "kcol", "qrow"), None), P(("groups", "kcol"), None), P("groups", None))
    return jax.shard_map(
        per_device,
        mesh=mesh,
        in_specs=placed,
        out_specs=P(("groups", "kcol", "qrow"), None),
        check_vma=False,
    )
```

profile of v0, /device:TPU:0, one launch (start us, length us, event | category | flops | bytes accessed | tf_op | source)
XLA Modules:
  0.0 169.5 jit_solution(10916630586948243898)
XLA Ops:
  6.6 0.8 compare_reduce_fusion.5
  7.4 0.7 fusion.37
  8.1 43.3 %all-gather.3 = bf16[16,4,1024]{2,1,0:T(4,128)(2,1)S(1)} all-gather(bf16[1,4,1024]{2,1,0:T(4,128)(2,1)} %bitcast.104), channel_id=1, replica_groups=mesh['groups'=1,'kcol'=16,'qrow'=2] {'kcol'}, dimensions={0}, use_global_device_ids=true | all-gather | bytes 139264 | tf_op jit(solution)/shard_map/all_gather | solution.py:62
  51.5 4.5 %select_reduce_fusion = (pred[1536]{0:T(1024)(128)(4,1)S(1)}, pred[1536]{0:T(1024)(128)(4,1)S(1)}, pred[1536]{0:T(1024)(128)(4,1)S(1)}, pred[1536]{0:T(1024)(128...) fusion(pred[]{:T(512)} %bitcast.11, pred[]{:T(512)} %bitcast.12, pred[]{:T(512)} %bitcast.13, ...), kind=kLoop, calls=%fused_computation.28 | loop fusion | flops 29184 | bytes 21511 | tf_op jit(solution)/shard_map/while/body/eval_jaxpr/jit(_take)/gather | solution.py:79
  56.0 3.2 %fusion.29 = pred[1536]{0:T(1024)(128)(4,1)S(1)} fusion(pred[1536]{0:T(1024)(128)(4,1)S(1)} %get-tuple-element.267, pred[1536]{0:T(1024)(128)(4,1)S(1)} %get-tuple-element.266, pred[1536]{0:T(1024)(128)(4,1)S(1)} %get-tuple-element.265, pred[1536]{0:T(1024)(128)(4,1)S(1)} %get-tuple-element.263, pred[1536]{0:T(1024)(128)(4,1)S(1)} %get-tuple-element.264, ...), kind=kLoop, calls=%fused_computation.47 | loop fusion | flops 21504 | bytes 10757 | tf_op jit(solution)/shard_map/while/body/eval_jaxpr/jit(_take)/select_n | solution.py:79
  59.4 1.7 %fusion.38 = (f32[8,64]{1,0:T(8,128)S(1)}, f32[8,64,1536]{2,1,0:T(8,128)S(1)}) fusion(bf16[64,8,128]{2,1,0:T(8,128)(2,1)S(1)} %squeeze.51, bf16[1536,256]{1,0:T(8,128)(2,1)} %param.8, pred[64,1536]{1,0:T(8,128)(4,1)S(1)} %compare_and_fusion), kind=kOutput, calls=%fused_computation.65 | convolution fusion | flops 203685376 | bytes 3770368 | tf_op jit(solution)/shard_map/while/body/eval_jaxpr/thd,kd->htk/dot_general | solution.py:25
  61.1 1.3 fusion.13
  62.5 0.7 fusion.7
  63.2 36.2 %all-gather.5 = f32[16,64,8]{1,2,0:T(8,128)S(1)} all-gather(f32[1,64,8]{1,2,0:T(8,128)S(1)} %bitcast.103), channel_id=3, replica_groups=mesh['groups'=1,'kcol'=16,'qrow'=2] {'kcol'}, dimensions={0}, use_global_device_ids=true | all-gather | bytes 34816 | tf_op jit(solution)/shard_map/all_gather | solution.py:12
  99.4 39.0 %all-gather.4 = f32[16,64,8]{1,2,0:T(8,128)S(1)} all-gather(f32[1,64,8]{1,2,0:T(8,128)S(1)} %bitcast.102), channel_id=2, replica_groups=mesh['groups'=1,'kcol'=16,'qrow'=2] {'kcol'}, dimensions={0}, use_global_device_ids=true | all-gather | bytes 34816 | tf_op jit(solution)/shard_map/all_gather | solution.py:12
  138.4 1.0 slice.53
  139.6 22.3 %while.26 = (s32[]{:T(128)}, f32[64,8]{0,1:T(8,128)S(1)}, f32[64,8]{0,1:T(8,128)S(1)}, f32[64,8,128]{2,1,0:T(8,128)S(1)}, f32[16,64,8]{1,2,0:T(8,128)S(1)}, /*in...) while((s32[]{:T(128)}, f32[64,8]{0,1:T(8,128)S(1)}, ...), condition=%wide.region_4.5_spmd, body=%wide.region_3.4_spmd.sunk | while | flops 199685 | bytes 1339535 | solution.py:17
  139.8 1.0 constant_dynamic-slice_fusion.3
  140.7 0.3 fusion.42
  141.3 1.0 constant_dynamic-slice_fusion.3
  142.2 0.3 fusion.42
  142.7 1.0 constant_dynamic-slice_fusion.3
  143.7 0.3 fusion.42
  144.2 1.0 constant_dynamic-slice_fusion.3
  145.7 1.0 constant_dynamic-slice_fusion.3
  147.2 1.0 constant_dynamic-slice_fusion.3
  148.7 1.0 constant_dynamic-slice_fusion.3
  150.2 1.0 constant_dynamic-slice_fusion.3
  151.1 0.3 fusion.42
  151.7 1.0 constant_dynamic-slice_fusion.3
  153.1 1.0 constant_dynamic-slice_fusion.3
  154.6 1.0 constant_dynamic-slice_fusion.3
  156.1 1.0 constant_dynamic-slice_fusion.3
  157.6 1.0 constant_dynamic-slice_fusion.3
  159.1 1.0 constant_dynamic-slice_fusion.3
  160.6 1.0 constant_dynamic-slice_fusion.3
  162.1 0.6 copy.43
  (73 shorter events, 6.7 us)
Async XLA Ops:
  6.5 131.9 %all-gather.8.cloned.1.call-start = ((), (), s32[]{:S(2)}) async-start(), calls=%async_computation | async-start | bytes 4456448 | tf_op jit(solution)/shard_map/all_gather | solution.py:12
  51.5 9.6 %copy-start = (bf16[1536,256]{1,0:T(8,128)(2,1)S(1)}, bf16[1536,256]{1,0:T(8,128)(2,1)}, u32[]{:S(2)}) copy-start(bf16[1536,256]{1,0:T(8,128)(2,1)} %param.8) | copy-start | bytes 2359300
Sparse Core Ops, SparseCore 0:
  62.6 72.8 all-gather.7
where the time goes:
time: 170 us
  blocking collectives  119 us (70%)
  local copies, waits for them, and re-layouts  19.7 us (12%)
  other arithmetic  14.2 us (8%)
  between operations  13.5 us (8%)
  matrix products  3.06 us (2%)
    all_gather x2, blocking collectives, combined_all(): gathered = jax.tree.map(lambda a: lax.all_gather(a, axis), part)  75.2 us
    all_gather x1, blocking collectives, per_device(): gathered = lax.all_gather(queries, 'kcol', axis=0, tiled=True)  43.3 us
    dynamic_slice x18, local copies, waits for them, and re-layouts, take(): lax.dynamic_index_in_dim(a, source, 0, False)  15.5 us
    gather x1, other arithmetic, one_block(): usable = jnp.repeat(listed_here, BLK, total_repeat_length=stored * BLK)  4.49 us
    add x15, other arithmetic, combine_partials(): numer_left * scale_left[..., None] + numer_right * scale_right[..., None]  4.46 us
  transfers between devices with their start and end apart: 1, of which 0 were waited for; matrix products, arithmetic and copies ran while one was open for 0% of the time, Pallas kernels for 0%

commit v1 on v0

--- a/solution.py
+++ b/solution.py
@@ -59,7 +59,16 @@
     head_count = feature_count // head_dim
     stored = key_value.shape[0] // BLK
     all_blocks = stored * column_count
-    gathered = lax.all_gather(queries, "kcol", axis=0, tiled=True)
+    ways = lax.axis_size("kcol")
+    up = [(d, (d + 1) % ways) for d in range(ways)]
+    down = [(d, (d - 1) % ways) for d in range(ways)]
+    earlier, later = ([queries], [queries])
+    for _ in range(ways // 2):
+        earlier.append(lax.ppermute(earlier[-1], "kcol", up))
+    for _ in range((ways - 1) // 2):
+        later.append(lax.ppermute(later[-1], "kcol", down))
+    line = jnp.concatenate([*earlier[::-1], *later[1:]], axis=0)
+    gathered = jnp.roll(line, (lax.axis_index("kcol") - ways // 2) * queries.shape[0], axis=0)
     gathered_rows = gathered.shape[0]
     tile_rows = BLK // row_count
     query_blocks = gathered_rows // tile_rows

time: 170 us -> 183 us (1.076)
  blocking collectives: 119 us -> 75.3 us
  starting transfers between devices: 0.01 us -> 41.6 us
  other arithmetic: 14.2 us -> 28 us
  waiting for transfers between devices: 0.02 us -> 13 us
  local copies, waits for them, and re-layouts: 19.7 us -> 7.07 us
    all_gather x1 -> x0, blocking collectives: 43.3 us -> none  [per_device(): gathered = lax.all_gather(queries, 'kcol', axis=0, tiled=True)]
    ppermute x0 -> x15, starting transfers between devices: none -> 41.6 us  [the longest x7 38.6 us: per_device(): later.append(lax.ppermute(later[-1], 'kcol', down))]
    dynamic_slice x18 -> x3, local copies, waits for them, and re-layouts: 15.5 us -> 0.97 us  [take(): lax.dynamic_index_in_dim(a, source, 0, False)]
    add x15, other arithmetic: 4.46 us -> 18.1 us  [combine_partials(): numer_left * scale_left[..., None] + numer_right * scale_right[..., None]]
    ppermute x0 -> x15, waiting for transfers between devices: none -> 13 us  [the longest x8 8.62 us: per_device(): earlier.append(lax.ppermute(earlier[-1], 'kcol', up))]
    concatenate x0 -> x1, local copies, waits for them, and re-layouts: none -> 1.91 us  [per_device(): jnp.roll(line, (lax.axis_index('kcol') - ways // 2) * queries.shape[0], a...]
  transfers between devices with their start and end apart: 1 -> 16, of which waited for: 0 -> 8; matrix products, arithmetic and copies ran while one was open for 0% -> 6% of each run, Pallas kernels for 0% -> 0%
where the time goes in v1:
time: 183 us; the launch traced here: 182 us
  blocking collectives  75.3 us (41%)
  starting transfers between devices  41.6 us (23%)
  other arithmetic  28 us (15%)
  between operations  13.5 us (7%)
  waiting for transfers between devices  13 us (7%)
  local copies, waits for them, and re-layouts  7.07 us (4%)
  matrix products  3.45 us (2%)
    all_gather x2, blocking collectives, combined_all(): gathered = jax.tree.map(lambda a: lax.all_gather(a, axis), part)  75.3 us
    ppermute x7, starting transfers between devices, per_device(): later.append(lax.ppermute(later[-1], 'kcol', down))  38.6 us
    add x15, other arithmetic, combine_partials(): numer_left * scale_left[..., None] + numer_right * scale_right[..., None]  18.1 us
    ppermute x8, waiting for transfers between devices, per_device(): earlier.append(lax.ppermute(earlier[-1], 'kcol', up))  8.62 us
    gather x1, other arithmetic, one_block(): usable = jnp.repeat(listed_here, BLK, total_repeat_length=stored * BLK)  4.42 us
    ppermute x7, waiting for transfers between devices, per_device(): later.append(lax.ppermute(later[-1], 'kcol', down))  4.4 us
  transfers between devices with their start and end apart: 16, of which 8 were waited for; matrix products, arithmetic and copies ran while one was open for 6% of the time, Pallas kernels for 0%

profile of v1, /device:TPU:0, one launch (start us, length us, event | category | flops | bytes accessed | tf_op | source)
XLA Modules:
  0.0 182.4 jit_solution(17181877227678484303)
XLA Ops:
  6.5 3.0 %collective-permute-start = (bf16[4,1024]{1,0:T(4,128)(2,1)}, bf16[4,1024]{1,0:T(4,128)(2,1)S(1)}, u32[]{:S(2)}, u32[]{:S(2)}) collective-permute-start(bf16[4,1024]{1,0:T(4,128)(2,1)} %param.7), channel_id=1, source_target_pairs={{0,2},{2,4},{4,6},{6,8},{8,10},{10,12},{12,14},{14,16},{16,18},{18... | collective-permute-start | bytes 24584 | tf_op jit(solution)/shard_map/ppermute | solution.py:67
  9.5 4.0 %collective-permute-start.8 = (bf16[4,1024]{1,0:T(4,128)(2,1)}, bf16[4,1024]{1,0:T(4,128)(2,1)S(1)}, u32[]{:S(2)}, u32[]{:S(2)}) collective-permute-start(bf16[4,1024]{1,0:T(4,128)(2,1)} %param.7), channel_id=1, source_target_pairs={{0,30},{2,0},{4,2},{6,4},{8,6},{10,8},{12,10},{14,12},{16,14},{18,... | collective-permute-start | bytes 24584 | tf_op jit(solution)/shard_map/ppermute | solution.py:69
  16.0 5.7 %collective-permute-start.9 = (bf16[4,1024]{1,0:T(4,128)(2,1)S(1)}, bf16[4,1024]{1,0:T(4,128)(2,1)S(1)}, u32[]{:S(2)}, u32[]{:S(2)}) collective-permute-start(bf16[4,1024]{1,0:T(4,128)(2,1)S(1)} %collective-permute-done.8), channel_id=1, source_target_pairs={{0,30},{2,0},{4,2},{6,4},{8,6},{10,8},{12,10},{14,12},{16,14},{18,... | collective-permute-start | bytes 24584 | tf_op jit(solution)/shard_map/ppermute | solution.py:69
  23.1 5.9 %collective-permute-start.10 = (bf16[4,1024]{1,0:T(4,128)(2,1)S(1)}, bf16[4,1024]{1,0:T(4,128)(2,1)S(1)}, u32[]{:S(2)}, u32[]{:S(2)}) collective-permute-start(bf16[4,1024]{1,0:T(4,128)(2,1)S(1)} %collective-permute-done.9), channel_id=1, source_target_pairs={{0,30},{2,0},{4,2},{6,4},{8,6},{10,8},{12,10},{14,12},{16,14},{18,... | collective-permute-start | bytes 24584 | tf_op jit(solution)/shard_map/ppermute | solution.py:69
  29.8 4.4 %select_reduce_fusion = (pred[1536]{0:T(1024)(128)(4,1)S(1)}, pred[1536]{0:T(1024)(128)(4,1)S(1)}, pred[1536]{0:T(1024)(128)(4,1)S(1)}, pred[1536]{0:T(1024)(128...) fusion(pred[]{:T(512)} %bitcast.11, pred[]{:T(512)} %bitcast.12, pred[]{:T(512)} %bitcast.13, ...), kind=kLoop, calls=%fused_computation.26 | loop fusion | flops 29184 | bytes 21511 | tf_op jit(solution)/shard_map/while/body/eval_jaxpr/jit(_take)/gather | solution.py:88
  34.3 5.7 %collective-permute-start.11 = (bf16[4,1024]{1,0:T(4,128)(2,1)S(1)}, bf16[4,1024]{1,0:T(4,128)(2,1)S(1)}, u32[]{:S(2)}, u32[]{:S(2)}) collective-permute-start(bf16[4,1024]{1,0:T(4,128)(2,1)S(1)} %collective-permute-done.10), channel_id=1, source_target_pairs={{0,30},{2,0},{4,2},{6,4},{8,6},{10,8},{12,10},{14,12},{16,14},{18,... | collective-permute-start | bytes 24584 | tf_op jit(solution)/shard_map/ppermute | solution.py:69
  39.9 3.2 %fusion.27 = pred[1536]{0:T(1024)(128)(4,1)S(1)} fusion(pred[1536]{0:T(1024)(128)(4,1)S(1)} %get-tuple-element.253, pred[1536]{0:T(1024)(128)(4,1)S(1)} %get-tuple-element.252, pred[1536]{0:T(1024)(128)(4,1)S(1)} %get-tuple-element.251, pred[1536]{0:T(1024)(128)(4,1)S(1)} %get-tuple-element.249, pred[1536]{0:T(1024)(128)(4,1)S(1)} %get-tuple-element.250, ...), kind=kLoop, calls=%fused_computation.45 | loop fusion | flops 21504 | bytes 10757 | tf_op jit(solution)/shard_map/while/body/eval_jaxpr/jit(_take)/select_n | solution.py:88
  43.2 5.7 %collective-permute-start.12 = (bf16[4,1024]{1,0:T(4,128)(2,1)S(1)}, bf16[4,1024]{1,0:T(4,128)(2,1)S(1)}, u32[]{:S(2)}, u32[]{:S(2)}) collective-permute-start(bf16[4,1024]{1,0:T(4,128)(2,1)S(1)} %collective-permute-done.11), channel_id=1, source_target_pairs={{0,30},{2,0},{4,2},{6,4},{8,6},{10,8},{12,10},{14,12},{16,14},{18,... | collective-permute-start | bytes 24584 | tf_op jit(solution)/shard_map/ppermute | solution.py:69
  48.9 1.4 collective-permute-done.12
  50.2 5.9 %collective-permute-start.13 = (bf16[4,1024]{1,0:T(4,128)(2,1)S(1)}, bf16[4,1024]{1,0:T(4,128)(2,1)S(1)}, u32[]{:S(2)}, u32[]{:S(2)}) collective-permute-start(bf16[4,1024]{1,0:T(4,128)(2,1)S(1)} %collective-permute-done.12), channel_id=1, source_target_pairs={{0,30},{2,0},{4,2},{6,4},{8,6},{10,8},{12,10},{14,12},{16,14},{18,... | collective-permute-start | bytes 24584 | tf_op jit(solution)/shard_map/ppermute | solution.py:69
  56.1 1.4 collective-permute-done.13
  57.5 5.9 %collective-permute-start.14 = (bf16[4,1024]{1,0:T(4,128)(2,1)S(1)}, bf16[4,1024]{1,0:T(4,128)(2,1)S(1)}, u32[]{:S(2)}, u32[]{:S(2)}) collective-permute-start(bf16[4,1024]{1,0:T(4,128)(2,1)S(1)} %collective-permute-done.13), channel_id=1, source_target_pairs={{0,30},{2,0},{4,2},{6,4},{8,6},{10,8},{12,10},{14,12},{16,14},{18,... | collective-permute-start | bytes 24584 | tf_op jit(solution)/shard_map/ppermute | solution.py:69
  64.7 5.9 %collective-permute-done.7 = bf16[4,1024]{1,0:T(4,128)(2,1)S(1)} collective-permute-done((bf16[4,1024]{1,0:T(4,128)(2,1)S(1)}, bf16[4,1024]{1,0:T(4,128)(2,1)S(1)}, u32[]{:S(2)}, u32[]{:S(2)}) %collective-permute-start.7) | collective-permute-done | bytes 8224 | tf_op jit(solution)/shard_map/ppermute | solution.py:67
  70.6 1.9 %concatenate.12 = bf16[128,1024]{1,0:T(8,128)(2,1)S(1)} concatenate(bf16[4,1024]{1,0:T(4,128)(2,1)S(1)} %collective-permute-done.7, bf16[4,1024]{1,0:T(4,128)(2,1)S(1)} %collective-permute-done.6, bf16[4,1024]{1,0:T(4,128)(2,1)S(1)} %collective-permute-done.5, bf16[4,1024]{1,0:T(4,128)(2,1)S(1)} %collective-permute-done.4, bf16[4,1024]{1,0:T(4,128)(2,1)S(1)} %collective-permute-done.3, ...), dimensions={0} | concatenate | bytes 524288 | tf_op jit(solution)/shard_map/jit(_roll_dynamic)/concatenate | solution.py:71
  72.6 2.0 %fusion.36 = (f32[8,64]{0,1:T(8,128)S(1)}, f32[8,64,1536]{2,0,1:T(8,128)S(1)}) fusion(bf16[64,8,128]{2,1,0:T(8,128)(2,1)S(1)} %bitcast.101, bf16[1536,256]{1,0:T(8,128)(2,1)} %param.8, pred[64,1536]{1,0:T(8,128)(4,1)S(1)} %compare_and_fusion), kind=kOutput, calls=%fused_computation.63 | convolution fusion | flops 203685376 | bytes 3770368 | tf_op jit(solution)/shard_map/while/body/eval_jaxpr/thd,kd->htk/dot_general | solution.py:25
  74.6 1.5 fusion.12
  77.1 36.2 %all-gather.4 = f32[16,64,8]{1,2,0:T(8,128)S(1)} all-gather(f32[1,64,8]{1,2,0:T(8,128)S(1)} %copy.27), channel_id=3, replica_groups=mesh['groups'=1,'kcol'=16,'qrow'=2] {'kcol'}, dimensions={0}, use_global_device_ids=true | all-gather | bytes 34816 | tf_op jit(solution)/shard_map/all_gather | solution.py:12
  113.3 39.1 %all-gather.3 = f32[16,64,8]{1,2,0:T(8,128)S(1)} all-gather(f32[1,64,8]{1,2,0:T(8,128)S(1)} %copy.26), channel_id=2, replica_groups=mesh['groups'=1,'kcol'=16,'qrow'=2] {'kcol'}, dimensions={0}, use_global_device_ids=true | all-gather | bytes 34816 | tf_op jit(solution)/shard_map/all_gather | solution.py:12
  153.4 21.3 %while.26 = (s32[]{:T(128)}, f32[64,8]{0,1:T(8,128)S(1)}, f32[64,8]{0,1:T(8,128)S(1)}, f32[64,8,128]{2,1,0:T(8,128)S(1)}, f32[16,64,8]{1,2,0:T(8,128)S(1)}, /*in...) while((s32[]{:T(128)}, f32[64,8]{0,1:T(8,128)S(1)}, ...), condition=%wide.region_4.5_spmd, body=%wide.region_3.4_spmd.sunk | while | flops 199685 | bytes 815247 | solution.py:17
  153.6 1.2 fusion.41
  155.0 1.2 fusion.41
  156.4 1.2 fusion.41
  157.8 1.2 fusion.41
  159.3 1.2 fusion.41
  160.7 1.2 fusion.41
  162.1 1.2 fusion.41
  163.5 1.2 fusion.41
  164.9 1.2 fusion.41
  166.4 1.2 fusion.41
  167.8 1.2 fusion.41
  169.2 1.2 fusion.41
  170.6 1.2 fusion.41
  (90 shorter events, 14.3 us)
Async XLA Ops:
  6.5 145.9 %all-gather.7.cloned.1.call-start = ((), (), s32[]{:S(2)}) async-start(), calls=%async_computation | async-start | bytes 4456448 | tf_op jit(solution)/shard_map/all_gather | solution.py:12
  6.5 8.8 %collective-permute-start = (bf16[4,1024]{1,0:T(4,128)(2,1)}, bf16[4,1024]{1,0:T(4,128)(2,1)S(1)}, u32[]{:S(2)}, u32[]{:S(2)}) collective-permute-start(bf16[4,1024]{1,0:T(4,128)(2,1)} %param.7), channel_id=1, source_target_pairs={{0,2},{2,4},{4,6},{6,8},{8,10},{10,12},{12,14},{14,16},{16,18},{18... | collective-permute-start | bytes 24584 | tf_op jit(solution)/shard_map/ppermute | solution.py:67
  9.5 6.5 %collective-permute-start.8 = (bf16[4,1024]{1,0:T(4,128)(2,1)}, bf16[4,1024]{1,0:T(4,128)(2,1)S(1)}, u32[]{:S(2)}, u32[]{:S(2)}) collective-permute-start(bf16[4,1024]{1,0:T(4,128)(2,1)} %param.7), channel_id=1, source_target_pairs={{0,30},{2,0},{4,2},{6,4},{8,6},{10,8},{12,10},{14,12},{16,14},{18,... | collective-permute-start | bytes 24584 | tf_op jit(solution)/shard_map/ppermute | solution.py:69
  15.3 7.2 %collective-permute-start.1 = (bf16[4,1024]{1,0:T(4,128)(2,1)S(1)}, bf16[4,1024]{1,0:T(4,128)(2,1)S(1)}, u32[]{:S(2)}, u32[]{:S(2)}) collective-permute-start(bf16[4,1024]{1,0:T(4,128)(2,1)S(1)} %collective-permute-done), channel_id=1, source_target_pairs={{0,2},{2,4},{4,6},{6,8},{8,10},{10,12},{12,14},{14,16},{16,18},{18... | collective-permute-start | bytes 24584 | tf_op jit(solution)/shard_map/ppermute | solution.py:67
  16.0 7.0 %collective-permute-start.9 = (bf16[4,1024]{1,0:T(4,128)(2,1)S(1)}, bf16[4,1024]{1,0:T(4,128)(2,1)S(1)}, u32[]{:S(2)}, u32[]{:S(2)}) collective-permute-start(bf16[4,1024]{1,0:T(4,128)(2,1)S(1)} %collective-permute-done.8), channel_id=1, source_target_pairs={{0,30},{2,0},{4,2},{6,4},{8,6},{10,8},{12,10},{14,12},{16,14},{18,... | collective-permute-start | bytes 24584 | tf_op jit(solution)/shard_map/ppermute | solution.py:69
  22.6 7.2 %collective-permute-start.2 = (bf16[4,1024]{1,0:T(4,128)(2,1)S(1)}, bf16[4,1024]{1,0:T(4,128)(2,1)S(1)}, u32[]{:S(2)}, u32[]{:S(2)}) collective-permute-start(bf16[4,1024]{1,0:T(4,128)(2,1)S(1)} %collective-permute-done.1), channel_id=1, source_target_pairs={{0,2},{2,4},{4,6},{6,8},{8,10},{10,12},{12,14},{14,16},{16,18},{18... | collective-permute-start | bytes 24584 | tf_op jit(solution)/shard_map/ppermute | solution.py:67
  23.1 11.2 %collective-permute-start.10 = (bf16[4,1024]{1,0:T(4,128)(2,1)S(1)}, bf16[4,1024]{1,0:T(4,128)(2,1)S(1)}, u32[]{:S(2)}, u32[]{:S(2)}) collective-permute-start(bf16[4,1024]{1,0:T(4,128)(2,1)S(1)} %collective-permute-done.9), channel_id=1, source_target_pairs={{0,30},{2,0},{4,2},{6,4},{8,6},{10,8},{12,10},{14,12},{16,14},{18,... | collective-permute-start | bytes 24584 | tf_op jit(solution)/shard_map/ppermute | solution.py:69
  29.8 10.1 %collective-permute-start.3 = (bf16[4,1024]{1,0:T(4,128)(2,1)S(1)}, bf16[4,1024]{1,0:T(4,128)(2,1)S(1)}, u32[]{:S(2)}, u32[]{:S(2)}) collective-permute-start(bf16[4,1024]{1,0:T(4,128)(2,1)S(1)} %collective-permute-done.2), channel_id=1, source_target_pairs={{0,2},{2,4},{4,6},{6,8},{8,10},{10,12},{12,14},{14,16},{16,18},{18... | collective-permute-start | bytes 24584 | tf_op jit(solution)/shard_map/ppermute | solution.py:67
  34.3 8.9 %collective-permute-start.11 = (bf16[4,1024]{1,0:T(4,128)(2,1)S(1)}, bf16[4,1024]{1,0:T(4,128)(2,1)S(1)}, u32[]{:S(2)}, u32[]{:S(2)}) collective-permute-start(bf16[4,1024]{1,0:T(4,128)(2,1)S(1)} %collective-permute-done.10), channel_id=1, source_target_pairs={{0,30},{2,0},{4,2},{6,4},{8,6},{10,8},{12,10},{14,12},{16,14},{18,... | collective-permute-start | bytes 24584 | tf_op jit(solution)/shard_map/ppermute | solution.py:69
  39.9 8.9 %collective-permute-start.4 = (bf16[4,1024]{1,0:T(4,128)(2,1)S(1)}, bf16[4,1024]{1,0:T(4,128)(2,1)S(1)}, u32[]{:S(2)}, u32[]{:S(2)}) collective-permute-start(bf16[4,1024]{1,0:T(4,128)(2,1)S(1)} %collective-permute-done.3), channel_id=1, source_target_pairs={{0,2},{2,4},{4,6},{6,8},{8,10},{10,12},{12,14},{14,16},{16,18},{18... | collective-permute-start | bytes 24584 | tf_op jit(solution)/shard_map/ppermute | solution.py:67
  43.2 7.0 %collective-permute-start.12 = (bf16[4,1024]{1,0:T(4,128)(2,1)S(1)}, bf16[4,1024]{1,0:T(4,128)(2,1)S(1)}, u32[]{:S(2)}, u32[]{:S(2)}) collective-permute-start(bf16[4,1024]{1,0:T(4,128)(2,1)S(1)} %collective-permute-done.11), channel_id=1, source_target_pairs={{0,30},{2,0},{4,2},{6,4},{8,6},{10,8},{12,10},{14,12},{16,14},{18,... | collective-permute-start | bytes 24584 | tf_op jit(solution)/shard_map/ppermute | solution.py:69
  48.9 7.2 %collective-permute-start.5 = (bf16[4,1024]{1,0:T(4,128)(2,1)S(1)}, bf16[4,1024]{1,0:T(4,128)(2,1)S(1)}, u32[]{:S(2)}, u32[]{:S(2)}) collective-permute-start(bf16[4,1024]{1,0:T(4,128)(2,1)S(1)} %collective-permute-done.4), channel_id=1, source_target_pairs={{0,2},{2,4},{4,6},{6,8},{8,10},{10,12},{12,14},{14,16},{16,18},{18... | collective-permute-start | bytes 24584 | tf_op jit(solution)/shard_map/ppermute | solution.py:67
  50.2 7.2 %collective-permute-start.13 = (bf16[4,1024]{1,0:T(4,128)(2,1)S(1)}, bf16[4,1024]{1,0:T(4,128)(2,1)S(1)}, u32[]{:S(2)}, u32[]{:S(2)}) collective-permute-start(bf16[4,1024]{1,0:T(4,128)(2,1)S(1)} %collective-permute-done.12), channel_id=1, source_target_pairs={{0,30},{2,0},{4,2},{6,4},{8,6},{10,8},{12,10},{14,12},{16,14},{18,... | collective-permute-start | bytes 24584 | tf_op jit(solution)/shard_map/ppermute | solution.py:69
  56.1 7.2 %collective-permute-start.6 = (bf16[4,1024]{1,0:T(4,128)(2,1)S(1)}, bf16[4,1024]{1,0:T(4,128)(2,1)S(1)}, u32[]{:S(2)}, u32[]{:S(2)}) collective-permute-start(bf16[4,1024]{1,0:T(4,128)(2,1)S(1)} %collective-permute-done.5), channel_id=1, source_target_pairs={{0,2},{2,4},{4,6},{6,8},{8,10},{10,12},{12,14},{14,16},{16,18},{18... | collective-permute-start | bytes 24584 | tf_op jit(solution)/shard_map/ppermute | solution.py:67
  57.5 7.2 %collective-permute-start.14 = (bf16[4,1024]{1,0:T(4,128)(2,1)S(1)}, bf16[4,1024]{1,0:T(4,128)(2,1)S(1)}, u32[]{:S(2)}, u32[]{:S(2)}) collective-permute-start(bf16[4,1024]{1,0:T(4,128)(2,1)S(1)} %collective-permute-done.13), channel_id=1, source_target_pairs={{0,30},{2,0},{4,2},{6,4},{8,6},{10,8},{12,10},{14,12},{16,14},{18,... | collective-permute-start | bytes 24584 | tf_op jit(solution)/shard_map/ppermute | solution.py:69
  63.3 7.2 %collective-permute-start.7 = (bf16[4,1024]{1,0:T(4,128)(2,1)S(1)}, bf16[4,1024]{1,0:T(4,128)(2,1)S(1)}, u32[]{:S(2)}, u32[]{:S(2)}) collective-permute-start(bf16[4,1024]{1,0:T(4,128)(2,1)S(1)} %collective-permute-done.6), channel_id=1, source_target_pairs={{0,2},{2,4},{4,6},{6,8},{8,10},{10,12},{12,14},{14,16},{16,18},{18... | collective-permute-start | bytes 24584 | tf_op jit(solution)/shard_map/ppermute | solution.py:67
  72.5 2.1 %copy-start = (bf16[1536,256]{1,0:T(8,128)(2,1)S(1)}, bf16[1536,256]{1,0:T(8,128)(2,1)}, u32[]{:S(2)}) copy-start(bf16[1536,256]{1,0:T(8,128)(2,1)} %param.8) | copy-start | bytes 2359300
Sparse Core Ops, SparseCore 0:
  76.2 72.0 all-gather.6
